TPU v7x, 32 devices: a whole 2x2x4 slice. The times are simulated.
32 devices in a mesh: dp: 8 (over y, x, core), tensor: 4 (over z).
Axes of the slice: x: 2, y: 2, z: 4, core: 2. Of those that a mesh axis runs over, the one named last changes fastest.
Arguments:
- tokens: bfloat16 [4096, 4096], P(('dp', 'tensor')), may hold values from -120 to 120
- norm_gain: float32 [4096], replicated, may hold values from 0.5 to 1.5
- w_gate: bfloat16 [4096, 8192], P('dp', 'tensor'), may hold values from -0.09375 to 0.09375
- w_up: bfloat16 [4096, 8192], P('dp', 'tensor'), may hold values from -0.09375 to 0.09375
- probes: bfloat16 [4096, 2, 8192], P('dp', None, 'tensor'), may hold values from -0.09375 to 0.09375
- cotangent: bfloat16 [4096, 8192], P('dp', 'tensor'), may hold values from -6 to 6
Outputs:
- hvp: float32 [4096, 2, 8192], P('dp', None, 'tensor')
All inputs are finite; a program needn't handle non-finite values.
Results may differ from a plain program's by a relative error of at most 0.014.
Values may be sent and summed in bfloat16 or wider, within the bound.
A program may use at most 128 MiB of HBM per device.

v0:
```python
import math
import jax
import jax.numpy as jnp
from jax import lax
from jax.sharding import PartitionSpec as P


def normalize(tokens, norm_gain):
    values = tokens.astype(jnp.float32)
    inverse = lax.rsqrt(jnp.mean(values * values, axis=1, keepdims=True) + 1e-05)
    return (values * inverse * norm_gain).astype(jnp.bfloat16)


def curvature(gate_pre):
    logistic = jax.nn.sigmoid(gate_pre)
    return logistic * (1.0 - logistic) * (2.0 + gate_pre * (1.0 - 2.0 * logistic))


def per_device(tokens, norm_gain, w_gate, w_up, probes, cotangent):
    normed = lax.all_gather(normalize(tokens, norm_gain), "tensor", axis=0, tiled=True)
    row_count = normed.shape[0]
    local_depth, probe_count, local_units = probes.shape
    probe_width = probe_count * local_units

    def project(shard_piece):
        return jnp.dot(normed, shard_piece, preferred_element_type=jnp.float32)

    gate_pre = project(lax.all_gather(w_gate, "dp", axis=0, tiled=True))
    up_pre = project(lax.all_gather(w_up, "dp", axis=0, tiled=True))
    shard_piece = lax.all_gather(probes, "dp", axis=0, tiled=True)
    tangent = project(shard_piece.reshape(shard_piece.shape[0], probe_width))
    scale_factor = 1.0 / math.sqrt(row_count * lax.axis_size("dp"))
    weighting = cotangent.astype(jnp.float32) * curvature(gate_pre) * up_pre * scale_factor
    second = (weighting[:, None, :] * tangent.reshape(row_count, probe_count, local_units)).astype(
        jnp.bfloat16
    )
    second = second.reshape(row_count, probe_width)
    result = lax.psum_scatter(
        lax.dot_general(
            normed, second, (((0,), (0,)), ((), ())), preferred_element_type=jnp.float32
        ).astype(jnp.bfloat16),
        "dp",
        scatter_dimension=0,
        tiled=True,
    ).astype(jnp.float32)
    return result.reshape(local_depth, probe_count, local_units)


def solution(mesh):
    in_specs = (
        P(("dp", "tensor"), None),
        P(),
        P("dp", "tensor"),
        P("dp", "tensor"),
        P("dp", None, "tensor"),
        P("dp", "tensor"),
    )
    out_specs = P("dp", None, "tensor")
    return jax.shard_map(
        per_device, mesh=mesh, in_specs=in_specs, out_specs=out_specs, check_vma=False
    )
```

profile of v0, /device:TPU:0, one launch (start us, length us, event | category | flops | bytes accessed | tf_op | source)
XLA Modules:
  0.0 797.4 jit_solution(14628051146677067251)
XLA Ops:
  6.5 1.5 fusion.11
  8.1 2.5 fusion.13
  10.6 0.0 all-gather.5.cloned.1.call-update
  10.6 0.0 all-gather.7.cloned.1.call-start
  10.7 0.7 all-gather.7.cloned.1.call-update
  11.4 0.0 all-gather.9.cloned.1.call-start
  11.4 0.7 all-gather.9.cloned.1.call-update
  12.1 0.0 all-gather.11.cloned.1.call-start
  12.2 0.5 all-gather.11.cloned.1.call-update
  12.7 0.0 copy-start
  12.7 0.0 reduce-scatter.2.cloned.1.call-start
  12.7 81.5 %all-gather.5.cloned.1.call-done = bf16[512,4096]{1,0:T(8,128)(2,1)} async-done(((bf16[128,4096]{1,0:T(8,128)(2,1)}), bf16[512,4096]{1,0:T(8,128)(2,1)}) %all-gather.5.cloned.1.call-update) | async-done | bytes 4194320 | tf_op jit(solution)/shard_map/all_gather | solution.py:20
  94.2 90.1 %all-gather.7.cloned.1.call-done = bf16[4096,2048]{1,0:T(8,128)(2,1)} async-done(((bf16[512,2048]{1,0:T(8,128)(2,1)}), bf16[4096,2048]{1,0:T(8,128)(2,1)}) %all-gather.7.cloned.1.call-update) | async-done | bytes 16777232 | tf_op jit(solution)/shard_map/all_gather | solution.py:28
  184.4 14.9 %fusion.14 = f32[512,2048]{1,0:T(8,128)} fusion(bf16[512,4096]{1,0:T(8,128)(2,1)} %all-gather.5.cloned.1.call-done, bf16[4096,2048]{1,0:T(8,128)(2,1)} %all-gather.7.cloned.1.call-done), kind=kOutput, calls=%fused_computation.16 | convolution fusion | flops 8589934592 | bytes 25165824 | tf_op jit(solution)/shard_map/dot_general | solution.py:26
  199.3 76.8 %all-gather.9.cloned.1.call-done = bf16[4096,2048]{1,0:T(8,128)(2,1)} async-done(((bf16[512,2048]{1,0:T(8,128)(2,1)}), bf16[4096,2048]{1,0:T(8,128)(2,1)}) %all-gather.9.cloned.1.call-update) | async-done | bytes 16777232 | tf_op jit(solution)/shard_map/all_gather | solution.py:29
  276.0 17.0 %fusion.5 = f32[512,2048]{1,0:T(8,128)} fusion(f32[512,2048]{1,0:T(8,128)} %fusion.14, bf16[512,2048]{1,0:T(8,128)(2,1)S(1)} %copy-done, bf16[512,4096]{1,0:T(8,128)(2,1)} %all-gather.5.cloned.1.call-done, bf16[4096,2048]{1,0:T(8,128)(2,1)} %all-gather.9.cloned.1.call-done), kind=kOutput, calls=%fused_computation.8 | convolution fusion | flops 8604614656 | bytes 31457280 | tf_op jit(solution)/shard_map/dot_general | solution.py:26
  293.0 145.5 %all-gather.11.cloned.1.call-done = bf16[4096,2,2048]{2,1,0:T(2,128)(2,1)} async-done(((bf16[512,2,2048]{2,1,0:T(2,128)(2,1)}), bf16[4096,2,2048]{2,1,0:T(2,128)(2,1)}) %all-gather.11.cloned.1.call-update) | async-done | bytes 33554448 | tf_op jit(solution)/shard_map/all_gather | solution.py:30
  438.5 80.7 %copy.12 = bf16[4096,2,2048]{0,2,1:T(8,128)(2,1)} copy(bf16[4096,2,2048]{2,1,0:T(2,128)(2,1)} %all-gather.11.cloned.1.call-done) | data formatting | bytes 67108864 | tf_op jit(solution)/shard_map/reshape | solution.py:31
  519.2 24.2 %multiply_convert_fusion = bf16[512,2,2048]{2,0,1:T(8,128)(2,1)} fusion(f32[512,2048]{1,0:T(8,128)} %fusion.5, bf16[4096,2,2048]{0,2,1:T(8,128)(2,1)} %copy.12, bf16[512,4096]{1,0:T(8,128)(2,1)} %all-gather.5.cloned.1.call-done), kind=kOutput, calls=%fused_computation.3 | convolution fusion | flops 17184063488 | bytes 46137344 | tf_op jit(solution)/shard_map/dot_general | solution.py:26
  543.4 6.2 copy.11
  549.6 24.1 %convolution_convert_fusion = bf16[4096,4096]{1,0:T(8,128)(2,1)} fusion(bf16[512,4096]{1,0:T(8,128)(2,1)} %all-gather.5.cloned.1.call-done, bf16[512,4096]{0,1:T(8,128)(2,1)} %bitcast.21), kind=kOutput, calls=%fused_computation.2 | convolution fusion | flops 17196646400 | bytes 41943040 | tf_op jit(solution)/shard_map/dot_general | solution.py:39
  573.7 0.0 reduce-scatter.2.cloned.1.call-update
  573.7 205.6 %reduce-scatter.2.cloned.1.call-done = bf16[512,4096]{1,0:T(8,128)(2,1)} async-done(((bf16[4096,4096]{1,0:T(8,128)(2,1)}), bf16[512,4096]{1,0:T(8,128)(2,1)}) %reduce-scatter.2.cloned.1.call-update) | async-done | bytes 4194320 | tf_op jit(solution)/shard_map/reduce_scatter | solution.py:38
  779.4 11.5 %reshape.29 = f32[512,2,2048]{2,1,0:T(2,128)} reshape(bf16[512,4096]{1,0:T(8,128)(2,1)} %reduce-scatter.2.cloned.1.call-done) | data formatting | bytes 12582912 | tf_op jit(solution)/shard_map/reshape | solution.py:46
  (3 shorter events, 0.0 us)
Async XLA Ops:
  6.5 87.7 %all-gather.5.cloned.1.call-start = ((), (), s32[]{:S(2)}) async-start(), calls=%async_computation.1 | async-start | bytes 5242880 | tf_op jit(solution)/shard_map/all_gather | solution.py:20
  10.6 173.8 %all-gather.7.cloned.1.call-start = ((), (), s32[]{:S(2)}) async-start(), calls=%async_computation.2 | async-start | bytes 18874368 | tf_op jit(solution)/shard_map/all_gather | solution.py:28
  11.4 264.7 %all-gather.9.cloned.1.call-start = ((), (), s32[]{:S(2)}) async-start(), calls=%async_computation.3 | async-start | bytes 18874368 | tf_op jit(solution)/shard_map/all_gather | solution.py:29
  12.1 426.4 %all-gather.11.cloned.1.call-start = ((), (), s32[]{:S(2)}) async-start(), calls=%async_computation.4 | async-start | bytes 37748736 | tf_op jit(solution)/shard_map/all_gather | solution.py:30
  12.7 263.3 %copy-start = (bf16[512,2048]{1,0:T(8,128)(2,1)S(1)}, bf16[512,2048]{1,0:T(8,128)(2,1)}, u32[]{:S(2)}) copy-start(bf16[512,2048]{1,0:T(8,128)(2,1)} %param.11) | copy-start | bytes 6291460
  12.7 766.7 %reduce-scatter.2.cloned.1.call-start = ((), (), s32[]{:S(2)}) async-start(), calls=%async_computation.5 | async-start | bytes 37748736 | tf_op jit(solution)/shard_map/reduce_scatter | solution.py:38
Sparse Core Ops, SparseCore 0:
  10.7 83.4 all-gather.4
  96.1 88.2 all-gather.6
  186.3 89.7 all-gather.8
  277.8 160.6 all-gather.10
  573.9 205.4 reduce-scatter.1
where the time goes:
time: 800 us; the launch traced here: 797 us
  waiting for transfers between devices  601 us (75%)
  local copies, waits for them, and re-layouts  98.4 us (12%)
  matrix products  80.2 us (10%)
  between operations  13.2 us (2%)
    reduce_scatter x1, waiting for transfers between devices, per_device(): lax.psum_scatter(lax.dot_general(normed, second, (((0,), (0,)), ((), ()))...  206 us
    all_gather x1, waiting for transfers between devices, per_device(): shard_piece = lax.all_gather(probes, 'dp', axis=0, tiled=True)  145 us
    all_gather x1, waiting for transfers between devices, per_device(): gate_pre = project(lax.all_gather(w_gate, 'dp', axis=0, tiled=True))  90.1 us
    all_gather x1, waiting for transfers between devices, per_device(): lax.all_gather(normalize(tokens, norm_gain), 'tensor', axis=0, tiled=True)  81.5 us
    reshape x1, local copies, waits for them, and re-layouts, per_device(): tangent = project(shard_piece.reshape(shard_piece.shape[0], probe_width))  80.7 us
    all_gather x1, waiting for transfers between devices, per_device(): up_pre = project(lax.all_gather(w_up, 'dp', axis=0, tiled=True))  76.8 us
    dot_general x3, matrix products, project(): return jnp.dot(normed, shard_piece, preferred_element_type=jnp.float32)  56.1 us
    dot_general x1, matrix products, per_device(): lax.dot_general(normed, second, (((0,), (0,)), ((), ())), preferred_eleme...  24.1 us
  transfers between devices with their start and end apart: 5, of which 5 were waited for; matrix products, arithmetic and copies ran while one was open for 4% of the time, Pallas kernels for 0%

commit v1 on v0

--- a/solution.py
+++ b/solution.py
@@ -25,7 +25,34 @@
     def project(shard_piece):
         return jnp.dot(normed, shard_piece, preferred_element_type=jnp.float32)
 
-    gate_pre = project(lax.all_gather(w_gate, "dp", axis=0, tiled=True))
+    def feed_steps_all_for(s0, dim_at):
+        local_next, piece_next, base_arr = (
+            jax.lax.axis_size("dp"),
+            jax.lax.axis_index("dp"),
+            s0.shape[dim_at],
+        )
+        blocks_here = [at * local_next if d == dim_at else at for d, at in enumerate(s0.shape)]
+        known = lax.dynamic_update_slice_in_dim(
+            jnp.zeros(blocks_here, s0.dtype), s0, piece_next * base_arr, axis=dim_at
+        )
+        v_now = f_next = s0
+        for s in tuple(range(1, local_next // 2 + 1)):
+            v_now = jax.lax.ppermute(
+                v_now, "dp", [(d, (d + 1) % local_next) for d in range(local_next)]
+            )
+            known = lax.dynamic_update_slice_in_dim(
+                known, v_now, (piece_next - s) % local_next * base_arr, axis=dim_at
+            )
+            if 2 * s < local_next:
+                f_next = jax.lax.ppermute(
+                    f_next, "dp", [(d, (d - 1) % local_next) for d in range(local_next)]
+                )
+                known = lax.dynamic_update_slice_in_dim(
+                    known, f_next, (piece_next + s) % local_next * base_arr, axis=dim_at
+                )
+        return known
+
+    gate_pre = project(feed_steps_all_for(w_gate, 0))
     up_pre = project(lax.all_gather(w_up, "dp", axis=0, tiled=True))
     shard_piece = lax.all_gather(probes, "dp", axis=0, tiled=True)
     tangent = project(shard_piece.reshape(shard_piece.shape[0], probe_width))

time: 800 us -> 761 us (0.951)
  waiting for transfers between devices: 601 us -> 526 us
  local copies, waits for them, and re-layouts: 98.4 us -> 124 us
  starting transfers between devices: 0.16 us -> 11.1 us
    ppermute x0 -> x7, waiting for transfers between devices: none -> 197 us  [the longest x4 188 us: feed_steps_all_for(): jax.lax.ppermute(v_now, 'dp', [(d, (d + 1) % local_next) for d in range(l...]
    all_gather x1 -> x0, waiting for transfers between devices: 90.1 us -> none  [per_device(): gate_pre = project(lax.all_gather(w_gate, 'dp', axis=0, tiled=True))]
    all_gather x1, waiting for transfers between devices: 81.5 us -> 0.01 us  [per_device(): lax.all_gather(normalize(tokens, norm_gain), 'tensor', axis=0, tiled=True)]
    all_gather x1, waiting for transfers between devices: 76.8 us -> 0.01 us  [per_device(): up_pre = project(lax.all_gather(w_up, 'dp', axis=0, tiled=True))]
    all_gather x1, waiting for transfers between devices: 145 us -> 122 us  [per_device(): shard_piece = lax.all_gather(probes, 'dp', axis=0, tiled=True)]
    dynamic_update_slice x0 -> x8, local copies, waits for them, and re-layouts: none -> 18.6 us  [the longest x4 9.27 us: feed_steps_all_for(): lax.dynamic_update_slice_in_dim(known, v_now, (piece_next - s) % local_ne...]
    ppermute x0 -> x7, starting transfers between devices: none -> 11 us  [the longest x3 9.05 us: feed_steps_all_for(): jax.lax.ppermute(f_next, 'dp', [(d, (d - 1) % local_next) for d in range(...]
  transfers between devices with their start and end apart: 5 -> 11, of which waited for: 5 -> 8; matrix products, arithmetic and copies ran while one was open for 4% -> 7% of each run, Pallas kernels for 0% -> 0%
where the time goes in v1:
time: 761 us; the launch traced here: 758 us
  waiting for transfers between devices  526 us (69%)
  local copies, waits for them, and re-layouts  124 us (16%)
  matrix products  79.5 us (10%)
  between operations  13.2 us (2%)
  starting transfers between devices  11.1 us (1%)
    reduce_scatter x1, waiting for transfers between devices, per_device(): lax.psum_scatter(lax.dot_general(normed, second, (((0,), (0,)), ((), ()))...  206 us
    ppermute x4, waiting for transfers between devices, feed_steps_all_for(): jax.lax.ppermute(v_now, 'dp', [(d, (d + 1) % local_next) for d in range(l...  188 us
    all_gather x1, waiting for transfers between devices, per_device(): shard_piece = lax.all_gather(probes, 'dp', axis=0, tiled=True)  122 us
    reshape x1, local copies, waits for them, and re-layouts, per_device(): tangent = project(shard_piece.reshape(shard_piece.shape[0], probe_width))  80.8 us
    dot_general x3, matrix products, project(): return jnp.dot(normed, shard_piece, preferred_element_type=jnp.float32)  55.3 us
    dot_general x1, matrix products, per_device(): lax.dot_general(normed, second, (((0,), (0,)), ((), ())), preferred_eleme...  24.2 us
  transfers between devices with their start and end apart: 11, of which 8 were waited for; matrix products, arithmetic and copies ran while one was open for 7% of the time, Pallas kernels for 0%

profile of v1, /device:TPU:0, one launch (start us, length us, event | category | flops | bytes accessed | tf_op | source)
XLA Modules:
  0.0 758.2 jit_solution(4498429646615686772)
XLA Ops:
  8.1 2.5 fusion.13
  12.7 2.9 collective-permute-start.1
  15.7 43.5 %collective-permute-done = bf16[512,2048]{1,0:T(8,128)(2,1)S(1)} collective-permute-done((bf16[512,2048]{1,0:T(8,128)(2,1)S(1)}, bf16[512,2048]{1,0:T(8,128)(2,1)S(1)}, u32[]{:S(2)}, u32[]{:S(2)}) %collective-permute-start) | collective-permute-done | bytes 2097184 | tf_op jit(solution)/shard_map/ppermute | solution.py:40
  60.7 3.2 collective-permute-start.3
  63.9 41.5 %collective-permute-done.2 = bf16[512,2048]{1,0:T(8,128)(2,1)S(1)} collective-permute-done((bf16[512,2048]{1,0:T(8,128)(2,1)S(1)}, bf16[512,2048]{1,0:T(8,128)(2,1)S(1)}, u32[]{:S(2)}, u32[]{:S(2)}) %collective-permute-start.2) | collective-permute-done | bytes 2097184 | tf_op jit(solution)/shard_map/ppermute | solution.py:40
  106.3 8.2 %collective-permute-done.3 = bf16[512,2048]{1,0:T(8,128)(2,1)} collective-permute-done((bf16[512,2048]{1,0:T(8,128)(2,1)S(1)}, bf16[512,2048]{1,0:T(8,128)(2,1)}, u32[]{:S(2)}, u32[]{:S(2)}) %collective-permute-start.3) | collective-permute-done | bytes 2097184 | tf_op jit(solution)/shard_map/ppermute | solution.py:47
  114.6 2.9 collective-permute-start.5
  117.5 73.1 %collective-permute-done.4 = bf16[512,2048]{1,0:T(8,128)(2,1)} collective-permute-done((bf16[512,2048]{1,0:T(8,128)(2,1)S(1)}, bf16[512,2048]{1,0:T(8,128)(2,1)}, u32[]{:S(2)}, u32[]{:S(2)}) %collective-permute-start.4) | collective-permute-done | bytes 2097184 | tf_op jit(solution)/shard_map/ppermute | solution.py:40
  190.5 6.0 broadcast_in_dim.2
  200.3 1.5 constant_dynamic-update-slice_fusion.5
  203.3 3.2 constant_dynamic-update-slice_fusion.3
  206.5 3.2 constant_dynamic-update-slice_fusion.2
  209.6 3.2 constant_dynamic-update-slice_fusion.1
  212.8 30.1 %collective-permute-done.6 = bf16[512,2048]{1,0:T(8,128)(2,1)} collective-permute-done((bf16[512,2048]{1,0:T(8,128)(2,1)}, bf16[512,2048]{1,0:T(8,128)(2,1)}, u32[]{:S(2)}, u32[]{:S(2)}) %collective-permute-start.6) | collective-permute-done | bytes 2097184 | tf_op jit(solution)/shard_map/ppermute | solution.py:40
  242.9 3.2 constant_dynamic-update-slice_fusion
  246.2 15.5 %fusion.14 = f32[512,2048]{1,0:T(8,128)S(1)} fusion(bf16[512,4096]{1,0:T(8,128)(2,1)} %all-gather.4.cloned.1.call-done, bf16[4096,2048]{1,0:T(8,128)(2,1)} %all-gather.6.cloned.1.call-done), kind=kOutput, calls=%fused_computation.24 | convolution fusion | flops 8589934592 | bytes 25165824 | tf_op jit(solution)/shard_map/dot_general | solution.py:26
  261.7 15.7 %fusion.5 = f32[512,2048]{1,0:T(8,128)} fusion(f32[512,2048]{1,0:T(8,128)S(1)} %fusion.14, bf16[512,2048]{1,0:T(8,128)(2,1)S(1)} %copy-done.8, bf16[512,4096]{1,0:T(8,128)(2,1)S(1)} %copy-done.7, bf16[4096,2048]{1,0:T(8,128)(2,1)} %constant_dynamic-update-slice_fusion), kind=kOutput, calls=%fused_computation.8 | convolution fusion | flops 8604614656 | bytes 31457280 | tf_op jit(solution)/shard_map/dot_general | solution.py:26
  277.4 121.8 %all-gather.8.cloned.1.call-done = bf16[4096,2,2048]{2,1,0:T(2,128)(2,1)} async-done(((bf16[512,2,2048]{2,1,0:T(2,128)(2,1)}), bf16[4096,2,2048]{2,1,0:T(2,128)(2,1)}) %all-gather.8.cloned.1.call-update) | async-done | bytes 33554448 | tf_op jit(solution)/shard_map/all_gather | solution.py:57
  399.2 80.8 %copy.12 = bf16[4096,2,2048]{0,2,1:T(8,128)(2,1)} copy(bf16[4096,2,2048]{2,1,0:T(2,128)(2,1)} %all-gather.8.cloned.1.call-done) | data formatting | bytes 67108864 | tf_op jit(solution)/shard_map/reshape | solution.py:58
  480.0 24.1 %multiply_convert_fusion = bf16[512,2,2048]{2,0,1:T(8,128)(2,1)} fusion(f32[512,2048]{1,0:T(8,128)} %fusion.5, bf16[4096,2,2048]{0,2,1:T(8,128)(2,1)} %copy.12, bf16[512,4096]{1,0:T(8,128)(2,1)} %all-gather.4.cloned.1.call-done), kind=kOutput, calls=%fused_computation.3 | convolution fusion | flops 17184063488 | bytes 46137344 | tf_op jit(solution)/shard_map/dot_general | solution.py:26
  504.1 6.2 copy.11
  510.3 24.2 %convolution_convert_fusion = bf16[4096,4096]{1,0:T(8,128)(2,1)} fusion(bf16[512,4096]{1,0:T(8,128)(2,1)} %all-gather.4.cloned.1.call-done, bf16[512,4096]{0,1:T(8,128)(2,1)} %bitcast.21), kind=kOutput, calls=%fused_computation.2 | convolution fusion | flops 17196646400 | bytes 41943040 | tf_op jit(solution)/shard_map/dot_general | solution.py:66
  534.5 205.6 %reduce-scatter.2.cloned.1.call-done = bf16[512,4096]{1,0:T(8,128)(2,1)} async-done(((bf16[4096,4096]{1,0:T(8,128)(2,1)}), bf16[512,4096]{1,0:T(8,128)(2,1)}) %reduce-scatter.2.cloned.1.call-update) | async-done | bytes 4194320 | tf_op jit(solution)/shard_map/reduce_scatter | solution.py:65
  740.1 11.5 %reshape.29 = f32[512,2,2048]{2,1,0:T(2,128)} reshape(bf16[512,4096]{1,0:T(8,128)(2,1)} %reduce-scatter.2.cloned.1.call-done) | data formatting | bytes 12582912 | tf_op jit(solution)/shard_map/reshape | solution.py:73
  (39 shorter events, 11.3 us)
Async XLA Ops:
  6.5 239.6 %all-gather.4.cloned.1.call-start = ((), (), s32[]{:S(2)}) async-start(), calls=%async_computation.1 | async-start | bytes 5242880 | tf_op jit(solution)/shard_map/all_gather | solution.py:20
  10.6 1.6 copy-start
  10.6 235.5 %all-gather.6.cloned.1.call-start = ((), (), s32[]{:S(2)}) async-start(), calls=%async_computation.2 | async-start | bytes 18874368 | tf_op jit(solution)/shard_map/all_gather | solution.py:56
  11.4 387.8 %all-gather.8.cloned.1.call-start = ((), (), s32[]{:S(2)}) async-start(), calls=%async_computation.3 | async-start | bytes 37748736 | tf_op jit(solution)/shard_map/all_gather | solution.py:57
  12.1 728.0 %reduce-scatter.2.cloned.1.call-start = ((), (), s32[]{:S(2)}) async-start(), calls=%async_computation.4 | async-start | bytes 37748736 | tf_op jit(solution)/shard_map/reduce_scatter | solution.py:65
  12.2 47.0 %collective-permute-start = (bf16[512,2048]{1,0:T(8,128)(2,1)S(1)}, bf16[512,2048]{1,0:T(8,128)(2,1)S(1)}, u32[]{:S(2)}, u32[]{:S(2)}) collective-permute-start(bf16[512,2048]{1,0:T(8,128)(2,1)S(1)} %copy-done), channel_id=1, source_target_pairs={{0,4},{4,8},{8,12},{12,16},{16,20},{20,24},{24,28},{28,0},{1,5},{5... | collective-permute-start | bytes 6291464 | tf_op jit(solution)/shard_map/ppermute | solution.py:40
  12.7 47.9 %collective-permute-start.1 = (bf16[512,2048]{1,0:T(8,128)(2,1)S(1)}, bf16[512,2048]{1,0:T(8,128)(2,1)S(1)}, u32[]{:S(2)}, u32[]{:S(2)}) collective-permute-start(bf16[512,2048]{1,0:T(8,128)(2,1)S(1)} %copy-done), channel_id=1, source_target_pairs={{0,28},{4,0},{8,4},{12,8},{16,12},{20,16},{24,20},{28,24},{1,29},{... | collective-permute-start | bytes 6291464 | tf_op jit(solution)/shard_map/ppermute | solution.py:47
  59.2 1.5 copy-start.1
  59.2 46.2 %collective-permute-start.2 = (bf16[512,2048]{1,0:T(8,128)(2,1)S(1)}, bf16[512,2048]{1,0:T(8,128)(2,1)S(1)}, u32[]{:S(2)}, u32[]{:S(2)}) collective-permute-start(bf16[512,2048]{1,0:T(8,128)(2,1)S(1)} %collective-permute-done), channel_id=1, source_target_pairs={{0,4},{4,8},{8,12},{12,16},{16,20},{20,24},{24,28},{28,0},{1,5},{5... | collective-permute-start | bytes 6291464 | tf_op jit(solution)/shard_map/ppermute | solution.py:40
  60.7 44.7 %copy-start.3 = (bf16[512,2048]{1,0:T(8,128)(2,1)}, bf16[512,2048]{1,0:T(8,128)(2,1)S(1)}, u32[]{:S(2)}) copy-start(bf16[512,2048]{1,0:T(8,128)(2,1)S(1)} %collective-permute-done.1) | copy-start | bytes 6291460
  60.7 53.9 %collective-permute-start.3 = (bf16[512,2048]{1,0:T(8,128)(2,1)S(1)}, bf16[512,2048]{1,0:T(8,128)(2,1)}, u32[]{:S(2)}, u32[]{:S(2)}) collective-permute-start(bf16[512,2048]{1,0:T(8,128)(2,1)S(1)} %collective-permute-done.1), channel_id=1, source_target_pairs={{0,28},{4,0},{8,4},{12,8},{16,12},{20,16},{24,20},{28,24},{1,29},{... | collective-permute-start | bytes 6291464 | tf_op jit(solution)/shard_map/ppermute | solution.py:47
  105.4 9.2 %copy-start.5 = (bf16[512,2048]{1,0:T(8,128)(2,1)}, bf16[512,2048]{1,0:T(8,128)(2,1)S(1)}, u32[]{:S(2)}) copy-start(bf16[512,2048]{1,0:T(8,128)(2,1)S(1)} %collective-permute-done.2) | copy-start | bytes 6291460
  105.4 85.1 %collective-permute-start.4 = (bf16[512,2048]{1,0:T(8,128)(2,1)S(1)}, bf16[512,2048]{1,0:T(8,128)(2,1)}, u32[]{:S(2)}, u32[]{:S(2)}) collective-permute-start(bf16[512,2048]{1,0:T(8,128)(2,1)S(1)} %collective-permute-done.2), channel_id=1, source_target_pairs={{0,4},{4,8},{8,12},{12,16},{16,20},{20,24},{24,28},{28,0},{1,5},{5... | collective-permute-start | bytes 6291464 | tf_op jit(solution)/shard_map/ppermute | solution.py:40
  114.6 95.1 %collective-permute-start.5 = (bf16[512,2048]{1,0:T(8,128)(2,1)}, bf16[512,2048]{1,0:T(8,128)(2,1)}, u32[]{:S(2)}, u32[]{:S(2)}) collective-permute-start(bf16[512,2048]{1,0:T(8,128)(2,1)} %collective-permute-done.3), channel_id=1, source_target_pairs={{0,28},{4,0},{8,4},{12,8},{16,12},{20,16},{24,20},{28,24},{1,29},{... | collective-permute-start | bytes 6291464 | tf_op jit(solution)/shard_map/ppermute | solution.py:47
  190.5 52.4 %collective-permute-start.6 = (bf16[512,2048]{1,0:T(8,128)(2,1)}, bf16[512,2048]{1,0:T(8,128)(2,1)}, u32[]{:S(2)}, u32[]{:S(2)}) collective-permute-start(bf16[512,2048]{1,0:T(8,128)(2,1)} %collective-permute-done.4), channel_id=1, source_target_pairs={{0,4},{4,8},{8,12},{12,16},{16,20},{20,24},{24,28},{28,0},{1,5},{5... | collective-permute-start | bytes 6291464 | tf_op jit(solution)/shard_map/ppermute | solution.py:40
  196.5 2.3 copy-start.2
  196.5 3.8 copy-start.4
  198.9 3.0 copy-start.6
  246.2 15.5 %copy-start.8 = (bf16[512,2048]{1,0:T(8,128)(2,1)S(1)}, bf16[512,2048]{1,0:T(8,128)(2,1)}, u32[]{:S(2)}) copy-start(bf16[512,2048]{1,0:T(8,128)(2,1)} %param.11) | copy-start | bytes 6291460
  246.2 15.5 %copy-start.7 = (bf16[512,4096]{1,0:T(8,128)(2,1)S(1)}, bf16[512,4096]{1,0:T(8,128)(2,1)}, u32[]{:S(2)}) copy-start(bf16[512,4096]{1,0:T(8,128)(2,1)} %all-gather.4.cloned.1.call-done) | copy-start | bytes 12582916
Sparse Core Ops, SparseCore 0:
  10.8 83.4 all-gather.3
  96.1 138.6 all-gather.5
  236.7 162.4 all-gather.7
  534.6 205.4 reduce-scatter.1
